TPU v7x, 32 devices: a whole 2x2x4 slice. The times are simulated.
32 devices in a mesh: group: 2 (over y), seq: 16 (over z, x, core).
Axes of the slice: x: 2, y: 2, z: 4, core: 2. Of those that a mesh axis runs over, the one named last changes fastest.
Arguments:
- queries: bfloat16 [4096, 4096], P(('group', 'seq')), parts along dimension 0, may hold values from -64 to 64
- key_vectors: bfloat16 [4096, 1024], P(('group', 'seq')), parts along dimension 0, may hold values from -2 to 2
- value_vectors: bfloat16 [4096, 1024], P(('group', 'seq')), parts along dimension 0, may hold values from -6 to 6
- grad_output: bfloat16 [4096, 4096], P(('group', 'seq')), parts along dimension 0, may hold values from -6 to 6
- document_ids: int32 [4096], P('group'), parts along dimension 0, may hold values from 0 to 3, never falling along the last dimension, each value on 1 to 1024 neighbouring positions
Outputs:
- attention_out: bfloat16 [4096, 4096], P(('group', 'seq')), parts along dimension 0
- grad_queries: bfloat16 [4096, 4096], P(('group', 'seq')), parts along dimension 0
- grad_keys: bfloat16 [4096, 1024], P(('group', 'seq')), parts along dimension 0
- grad_values: bfloat16 [4096, 1024], P(('group', 'seq')), parts along dimension 0
There are 2 independent parts, one for each index of `group`. A program takes and returns all parts, laid end to end along the dimension named above; each array names one. Nothing has to cross between parts.
Inputs may be any that keep to these rules, and one draw needn't show every extreme that they name: `document_ids`: document numbers never fall along positions; each document covers 1 to 1024 consecutive positions and one covers exactly 1024.
All inputs are finite; a program needn't handle non-finite values.
Results may differ from a plain program's by a relative error of at most 0.015.
Values may be sent and summed in bfloat16 or wider, within the bound.
No kernel may reach another device: no remote copies, remote signals or barrier semaphores. Data moves between devices by JAX's collectives and lax.ppermute only.
A program may use at most 128 MiB of HBM per device.

v0:
```python
import math
import jax
import jax.numpy as jnp
from jax import lax
from jax.sharding import PartitionSpec as P

H = 32
KV = 8
HD = 128
MOST = 1024


def shifted(block, axis, distance):
    devices = range(lax.axis_size(axis))
    route = [(i - distance, i) for i in devices if i - distance in devices]
    return lax.ppermute(block, axis, route)


def attend_block(query_block, grad_block, key_block, value_block, allowed):
    score_scale = 1.0 / math.sqrt(query_block.shape[-1])
    scores = (
        jnp.einsum("qgd,kd->gqk", query_block, key_block, preferred_element_type=jnp.float32)
        * score_scale
    )
    scores = jnp.where(allowed[None], scores, -1e30)
    row_max = jnp.max(scores, axis=-1, keepdims=True)
    weights = jnp.exp(scores - row_max)
    softmax = weights / jnp.sum(weights, axis=-1, keepdims=True)
    probs_low = softmax.astype(jnp.bfloat16)
    output = jnp.einsum(
        "gqk,kd->qgd", probs_low, value_block, preferred_element_type=jnp.float32
    ).astype(jnp.bfloat16)
    row_delta = jnp.sum(grad_block.astype(jnp.float32) * output.astype(jnp.float32), axis=-1)
    grad_probs = jnp.einsum(
        "qgd,kd->gqk", grad_block, value_block, preferred_element_type=jnp.float32
    )
    grad_scores = (softmax * (grad_probs - jnp.transpose(row_delta)[:, :, None])).astype(
        jnp.bfloat16
    )
    grad_query = (
        jnp.einsum("gqk,kd->qgd", grad_scores, key_block, preferred_element_type=jnp.float32)
        * score_scale
    ).astype(jnp.bfloat16)
    grad_key = (
        jnp.einsum("gqk,qgd->kd", grad_scores, query_block, preferred_element_type=jnp.float32)
        * score_scale
    )
    grad_value = jnp.einsum(
        "gqk,qgd->kd", probs_low, grad_block, preferred_element_type=jnp.float32
    )
    return (output, grad_query, grad_key, grad_value)


def on_device(queries, key_vectors, value_vectors, grad_output, document_ids):
    devices = lax.axis_size("seq")
    position = lax.axis_index("seq")
    local_rows = queries.shape[0]
    group = H // KV
    ratio = devices // KV
    slot_rows = local_rows // ratio
    block_len = slot_rows * devices
    block_rows = min(512, block_len)

    def to_slots(tensor, columns):
        return (
            tensor.reshape(ratio, slot_rows, KV, columns)
            .transpose(1, 2, 0, 3)
            .reshape(slot_rows, devices, columns)
        )

    def from_slots(tensor, columns):
        height = tensor.shape[0]
        return tensor.reshape(height, KV, ratio, columns).transpose(2, 0, 1, 3)

    query_send = to_slots(queries, group * HD)
    grad_send = to_slots(grad_output, group * HD)
    key_send = to_slots(key_vectors, HD)
    value_send = to_slots(value_vectors, HD)
    query_in, grad_in, key_in, value_in = (
        lax.all_to_all(query_send, "seq", split_axis=1, concat_axis=1, tiled=True),
        lax.all_to_all(grad_send, "seq", split_axis=1, concat_axis=1, tiled=True),
        lax.all_to_all(key_send, "seq", split_axis=1, concat_axis=1, tiled=True),
        lax.all_to_all(value_send, "seq", split_axis=1, concat_axis=1, tiled=True),
    )
    query_head = query_in.reshape(block_len, group, HD)
    grad_head = grad_in.reshape(block_len, group, HD)
    key_flat = key_in.reshape(-1, HD)
    value_flat = value_in.reshape(-1, HD)
    stacked = jnp.stack([key_flat, value_flat])
    previous = shifted(stacked, "seq", 1)
    key_window = jnp.concatenate([previous[0], key_flat], axis=0)
    value_window = jnp.concatenate([previous[1], value_flat], axis=0)
    start = position % ratio * block_len
    padded_ids = jnp.concatenate([jnp.full((MOST,), -1, jnp.int32), document_ids])
    column_ids_all = lax.dynamic_slice_in_dim(padded_ids, start, MOST + block_len)
    row_ids_all = lax.dynamic_slice_in_dim(document_ids, start, block_len)
    column_index = jnp.arange(block_rows + MOST, dtype=jnp.int32)[None, :]
    row_index = jnp.arange(block_rows, dtype=jnp.int32)[:, None]

    def one_block(step_index, totals):
        out_all, dq_all, key_grad, value_grad = totals
        offset = step_index * block_rows
        query_block = lax.dynamic_slice_in_dim(query_head, offset, block_rows, 0)
        grad_block = lax.dynamic_slice_in_dim(grad_head, offset, block_rows, 0)
        key_block = lax.dynamic_slice_in_dim(key_window, offset, block_rows + MOST, 0)
        value_block = lax.dynamic_slice_in_dim(value_window, offset, block_rows + MOST, 0)
        row_ids = lax.dynamic_slice_in_dim(row_ids_all, offset, block_rows)
        column_ids = lax.dynamic_slice_in_dim(column_ids_all, offset, block_rows + MOST)
        allowed = (row_ids[:, None] == column_ids[None, :]) & (column_index <= row_index + MOST)
        output, grad_query, grad_key, grad_value = attend_block(
            query_block, grad_block, key_block, value_block, allowed
        )
        out_all = lax.dynamic_update_slice_in_dim(out_all, output, offset, 0)
        dq_all = lax.dynamic_update_slice_in_dim(dq_all, grad_query, offset, 0)
        key_grad = lax.dynamic_update_slice_in_dim(
            key_grad,
            lax.dynamic_slice_in_dim(key_grad, offset, block_rows + MOST, 0) + grad_key,
            offset,
            0,
        )
        value_grad = lax.dynamic_update_slice_in_dim(
            value_grad,
            lax.dynamic_slice_in_dim(value_grad, offset, block_rows + MOST, 0) + grad_value,
            offset,
            0,
        )
        return (out_all, dq_all, key_grad, value_grad)

    initial = (
        jnp.zeros((block_len, group, HD), jnp.bfloat16),
        jnp.zeros((block_len, group, HD), jnp.bfloat16),
        jnp.zeros((MOST + block_len, HD), jnp.float32),
        jnp.zeros((MOST + block_len, HD), jnp.float32),
    )
    out_all, dq_all, key_grad, value_grad = lax.fori_loop(
        0, block_len // block_rows, one_block, initial
    )
    out_send = out_all.reshape(slot_rows, devices, group * HD)
    dq_send = dq_all.reshape(slot_rows, devices, group * HD)
    returned = shifted(
        jnp.stack([key_grad[:MOST], value_grad[:MOST]]).astype(jnp.bfloat16), "seq", -1
    ).astype(jnp.float32)
    key_own = key_grad[MOST:].at[block_len - MOST :].add(returned[0]).astype(jnp.bfloat16)
    value_own = value_grad[MOST:].at[block_len - MOST :].add(returned[1]).astype(jnp.bfloat16)
    out_back, dq_back, key_back, value_back = (
        lax.all_to_all(out_send, "seq", split_axis=1, concat_axis=1, tiled=True),
        lax.all_to_all(dq_send, "seq", split_axis=1, concat_axis=1, tiled=True),
        lax.all_to_all(
            key_own.reshape(slot_rows, devices, HD), "seq", split_axis=1, concat_axis=1, tiled=True
        ),
        lax.all_to_all(
            value_own.reshape(slot_rows, devices, HD),
            "seq",
            split_axis=1,
            concat_axis=1,
            tiled=True,
        ),
    )
    grad_keys = from_slots(key_back, HD).reshape(local_rows, KV * HD)
    grad_values = from_slots(value_back, HD).reshape(local_rows, KV * HD)
    attention_out = from_slots(out_back, group * HD).reshape(local_rows, H * HD)
    grad_queries = from_slots(dq_back, group * HD).reshape(local_rows, H * HD)
    return (attention_out, grad_queries, grad_keys, grad_values)


def solution(mesh):
    placed = (
        P(("group", "seq"), None),
        P(("group", "seq"), None),
        P(("group", "seq"), None),
        P(("group", "seq"), None),
        P("group"),
    )
    return jax.shard_map(
        on_device,
        mesh=mesh,
        in_specs=placed,
        out_specs=(
            P(("group", "seq"), None),
            P(("group", "seq"), None),
            P(("group", "seq"), None),
            P(("group", "seq"), None),
        ),
        check_vma=False,
    )
```

profile of v0, /device:TPU:11, one launch (start us, length us, event | category | flops | bytes accessed | tf_op | source)
XLA Modules:
  0.0 312.5 jit_solution(9346794623854736078)
XLA Ops:
  2.4 6.6 %all-to-all-start = ((bf16[64,16,128]{2,0,1:T(8,128)(2,1)}), bf16[64,16,128]{2,0,1:T(8,128)(2,1)S(1)}, u32[]{:S(2)}, u32[]{:S(2)}) async-start(bf16[64,16,128]{2,0,1:T(8,128)(2,1)} %bitcast.1), calls=%async_computation | async-start | bytes 524288 | tf_op jit(solution)/shard_map/all_to_all | solution.py:82
  10.7 6.2 %all-to-all-done = bf16[64,16,128]{2,0,1:T(8,128)(2,1)S(1)} async-done(((bf16[64,16,128]{2,0,1:T(8,128)(2,1)}), bf16[64,16,128]{2,0,1:T(8,128)(2,1)S(1)}, u32[]{:S(2)}, u32[]{:S(2)}) %all-to-all-start) | async-done | bytes 262176 | tf_op jit(solution)/shard_map/all_to_all | solution.py:82
  16.9 5.5 %all-to-all-start.1 = ((bf16[64,16,128]{2,0,1:T(8,128)(2,1)}), bf16[64,16,128]{2,0,1:T(8,128)(2,1)S(1)}, u32[]{:S(2)}, u32[]{:S(2)}) async-start(bf16[64,16,128]{2,0,1:T(8,128)(2,1)} %bitcast.4), calls=%async_computation.1 | async-start | bytes 524288 | tf_op jit(solution)/shard_map/all_to_all | solution.py:83
  22.5 1.6 copy.132
  25.4 5.0 %all-to-all-done.1 = bf16[64,16,128]{2,0,1:T(8,128)(2,1)S(1)} async-done(((bf16[64,16,128]{2,0,1:T(8,128)(2,1)}), bf16[64,16,128]{2,0,1:T(8,128)(2,1)S(1)}, u32[]{:S(2)}, u32[]{:S(2)}) %all-to-all-start.1) | async-done | bytes 262176 | tf_op jit(solution)/shard_map/all_to_all | solution.py:83
  30.4 5.7 %all-to-all-start.2 = ((bf16[64,16,512]{2,0,1:T(8,128)(2,1)}), bf16[64,16,512]{2,0,1:T(8,128)(2,1)S(1)}, u32[]{:S(2)}, u32[]{:S(2)}) async-start(bf16[64,16,512]{2,0,1:T(8,128)(2,1)} %bitcast.11), calls=%async_computation.2 | async-start | bytes 2097152 | tf_op jit(solution)/shard_map/all_to_all | solution.py:80
  36.1 1.6 copy.133
  39.1 21.9 %all-to-all-done.2 = bf16[64,16,512]{2,0,1:T(8,128)(2,1)S(1)} async-done(((bf16[64,16,512]{2,0,1:T(8,128)(2,1)}), bf16[64,16,512]{2,0,1:T(8,128)(2,1)S(1)}, u32[]{:S(2)}, u32[]{:S(2)}) %all-to-all-start.2) | async-done | bytes 1048608 | tf_op jit(solution)/shard_map/all_to_all | solution.py:80
  61.0 4.9 %all-to-all-start.3 = ((bf16[64,16,512]{2,0,1:T(8,128)(2,1)}), bf16[64,16,512]{2,0,1:T(8,128)(2,1)S(1)}, u32[]{:S(2)}, u32[]{:S(2)}) async-start(bf16[64,16,512]{2,0,1:T(8,128)(2,1)} %bitcast.13), calls=%async_computation.3 | async-start | bytes 2097152 | tf_op jit(solution)/shard_map/all_to_all | solution.py:81
  67.1 3.3 %collective-permute-start = (bf16[2,1024,128]{2,1,0:T(8,128)(2,1)}, bf16[2,1024,128]{2,1,0:T(8,128)(2,1)S(1)}, u32[]{:S(2)}, u32[]{:S(2)}) collective-permute-start(bf16[2,1024,128]{2,1,0:T(8,128)(2,1)} %pad_maximum_fusion), channel_id=1, source_target_pairs={{0,1},{1,2},{2,3},{3,4},{4,5},{5,6},{6,7},{7,8},{8,9},{9,10},{10,1... | collective-permute-start | bytes 1572872 | tf_op jit(solution)/shard_map/ppermute | solution.py:16
  70.5 24.4 %collective-permute-done = bf16[2,1024,128]{2,1,0:T(8,128)(2,1)S(1)} collective-permute-done((bf16[2,1024,128]{2,1,0:T(8,128)(2,1)}, bf16[2,1024,128]{2,1,0:T(8,128)(2,1)S(1)}, u32[]{:S(2)}, u32[]{:S(2)}) %collective-permute-start) | collective-permute-done | bytes 524320 | tf_op jit(solution)/shard_map/ppermute | solution.py:16
  95.9 1.5 copy.99
  97.4 2.2 reshape.215
  105.9 102.4 %while.24 = (s32[]{:T(128)}, bf16[1024,4,128]{2,1,0:T(4,128)(2,1)}, bf16[1024,4,128]{2,1,0:T(4,128)(2,1)}, f32[2048,128]{1,0:T(8,128)}, f32[2048,128]{1,0:T(8,12...) while((s32[]{:T(128)}, bf16[1024,4,128]{2,1,0:T(4,128)(2,1)}, ...), condition=%wide.region_4.5_spmd.clone, body=%wide.region_0.4_spmd.clone.sunk | while | flops 4874371072 | bytes 147394880 | solution.py:135
  107.1 1.8 fusion.81
  109.1 1.6 fusion.82
  110.7 10.0 %fusion.83 = (f32[4,512]{1,0:T(4,128)S(1)}, f32[4,512,1536]{1,2,0:T(8,128)}) fusion(f32[1536,512,4]{1,0,2:T(8,128)S(1)} %fusion.81, pred[512,1536]{0,1:T(8,128)(4,1)} %fusion.82), kind=kOutput, calls=%fused_computation.72.clone.1 | output fusion | flops 18875904 | bytes 25960448 | tf_op jit(solution)/shard_map/while/body/eval_jaxpr/sub | solution.py:27
  120.7 9.1 %fusion.84 = bf16[4,512,1536]{1,2,0:T(8,128)(2,1)} fusion(f32[4,512,1536]{1,2,0:T(8,128)} %get-tuple-element.452, f32[4,512]{1,0:T(4,128)S(1)} %get-tuple-element.453), kind=kLoop, calls=%fused_computation.13.clone.1 | loop fusion | flops 6291456 | bytes 18882560 | tf_op jit(solution)/shard_map/while/body/eval_jaxpr/convert_element_type | solution.py:29
  130.3 4.0 %multiply_reduce_fusion.2 = (f32[512,4]{0,1:T(4,128)S(1)}, bf16[512,4,128]{0,2,1:T(8,128)(2,1)S(1)}) fusion(bf16[512,4,128]{0,2,1:T(8,128)(2,1)S(1)} %copy.153, bf16[4,512,1536]{1,2,0:T(8,128)(2,1)} %fusion.84, bf16[2048,128]{1,0:T(8,128)(2,1)} %get-tuple-element.495, s32[]{:T(128)S(6)} %select_n.66), kind=kOutput, calls=%fused_computation.28.clone.1 | convolution fusion | flops 806615040 | bytes 7741444 | tf_op jit(solution)/shard_map/while/body/eval_jaxpr/gqk,kd->qgd/dot_general | solution.py:30
  134.2 5.9 %fusion.85 = bf16[4,512,1536]{1,2,0:T(8,128)(2,1)S(1)} fusion(bf16[512,4,128]{0,2,1:T(8,128)(2,1)S(1)} %copy.153, f32[4,512]{1,0:T(4,128)S(1)} %bitcast.201, f32[4,512,1536]{1,2,0:T(8,128)} %get-tuple-element.452, f32[4,512]{1,0:T(4,128)S(1)} %get-tuple-element.453, bf16[2048,128]{1,0:T(8,128)(2,1)} %get-tuple-element.495, s32[]{:T(128)S(6)} %select_n.66), kind=kOutput, calls=%fused_computation.5.clone.1 | convolution fusion | flops 817889280 | bytes 19808260 | tf_op jit(solution)/shard_map/while/body/eval_jaxpr/qgd,kd->gqk/dot_general | solution.py:34
  140.1 2.6 copy-done
  144.4 1.3 constant_dynamic-update-slice_fusion.3
  145.8 5.6 %fusion.87 = f32[2048,128]{1,0:T(8,128)} fusion(f32[2048,128]{1,0:T(8,128)} %get-tuple-element.477, s32[]{:T(128)S(6)} %select_n.66, bf16[4,512,1536]{1,2,0:T(8,128)(2,1)} %copy-done, bf16[512,4,128]{2,1,0:T(4,128)(2,1)S(1)} %constant_dynamic-slice_fusion.5), kind=kOutput, calls=%fused_computation.20.clone.1 | convolution fusion | flops 805699584 | bytes 8388612 | tf_op jit(solution)/shard_map/while/body/eval_jaxpr/gqk,qgd->kd/dot_general | solution.py:45
  151.4 5.6 %fusion.88 = f32[2048,128]{1,0:T(8,128)} fusion(f32[2048,128]{1,0:T(8,128)} %get-tuple-element.478, s32[]{:T(128)S(6)} %select_n.66, bf16[4,512,1536]{1,2,0:T(8,128)(2,1)} %fusion.84, bf16[512,4,128]{0,2,1:T(8,128)(2,1)S(1)} %copy.153), kind=kOutput, calls=%fused_computation.22.clone.1 | convolution fusion | flops 805502976 | bytes 8388612 | tf_op jit(solution)/shard_map/while/body/eval_jaxpr/gqk,qgd->kd/dot_general | solution.py:48
  158.3 1.8 fusion.81
  160.2 1.6 fusion.82
  161.8 10.0 %fusion.83 = (f32[4,512]{1,0:T(4,128)S(1)}, f32[4,512,1536]{1,2,0:T(8,128)}) fusion(f32[1536,512,4]{1,0,2:T(8,128)S(1)} %fusion.81, pred[512,1536]{0,1:T(8,128)(4,1)} %fusion.82), kind=kOutput, calls=%fused_computation.72.clone.1 | output fusion | flops 18875904 | bytes 25960448 | tf_op jit(solution)/shard_map/while/body/eval_jaxpr/sub | solution.py:27
  171.8 9.1 %fusion.84 = bf16[4,512,1536]{1,2,0:T(8,128)(2,1)} fusion(f32[4,512,1536]{1,2,0:T(8,128)} %get-tuple-element.452, f32[4,512]{1,0:T(4,128)S(1)} %get-tuple-element.453), kind=kLoop, calls=%fused_computation.13.clone.1 | loop fusion | flops 6291456 | bytes 18882560 | tf_op jit(solution)/shard_map/while/body/eval_jaxpr/convert_element_type | solution.py:29
  181.4 4.0 %multiply_reduce_fusion.2 = (f32[512,4]{0,1:T(4,128)S(1)}, bf16[512,4,128]{0,2,1:T(8,128)(2,1)S(1)}) fusion(bf16[512,4,128]{0,2,1:T(8,128)(2,1)S(1)} %copy.153, bf16[4,512,1536]{1,2,0:T(8,128)(2,1)} %fusion.84, bf16[2048,128]{1,0:T(8,128)(2,1)} %get-tuple-element.495, s32[]{:T(128)S(6)} %select_n.66), kind=kOutput, calls=%fused_computation.28.clone.1 | convolution fusion | flops 806615040 | bytes 7741444 | tf_op jit(solution)/shard_map/while/body/eval_jaxpr/gqk,kd->qgd/dot_general | solution.py:30
  185.4 5.9 %fusion.85 = bf16[4,512,1536]{1,2,0:T(8,128)(2,1)S(1)} fusion(bf16[512,4,128]{0,2,1:T(8,128)(2,1)S(1)} %copy.153, f32[4,512]{1,0:T(4,128)S(1)} %bitcast.201, f32[4,512,1536]{1,2,0:T(8,128)} %get-tuple-element.452, f32[4,512]{1,0:T(4,128)S(1)} %get-tuple-element.453, bf16[2048,128]{1,0:T(8,128)(2,1)} %get-tuple-element.495, s32[]{:T(128)S(6)} %select_n.66), kind=kOutput, calls=%fused_computation.5.clone.1 | convolution fusion | flops 817889280 | bytes 19808260 | tf_op jit(solution)/shard_map/while/body/eval_jaxpr/qgd,kd->gqk/dot_general | solution.py:34
  191.3 2.6 copy-done
  196.9 5.7 %fusion.87 = f32[2048,128]{1,0:T(8,128)} fusion(f32[2048,128]{1,0:T(8,128)} %get-tuple-element.477, s32[]{:T(128)S(6)} %select_n.66, bf16[4,512,1536]{1,2,0:T(8,128)(2,1)} %copy-done, bf16[512,4,128]{2,1,0:T(4,128)(2,1)S(1)} %constant_dynamic-slice_fusion.5), kind=kOutput, calls=%fused_computation.20.clone.1 | convolution fusion | flops 805699584 | bytes 8388612 | tf_op jit(solution)/shard_map/while/body/eval_jaxpr/gqk,qgd->kd/dot_general | solution.py:45
  202.6 5.7 %fusion.88 = f32[2048,128]{1,0:T(8,128)} fusion(f32[2048,128]{1,0:T(8,128)} %get-tuple-element.478, s32[]{:T(128)S(6)} %select_n.66, bf16[4,512,1536]{1,2,0:T(8,128)(2,1)} %fusion.84, bf16[512,4,128]{0,2,1:T(8,128)(2,1)S(1)} %copy.153), kind=kOutput, calls=%fused_computation.22.clone.1 | convolution fusion | flops 805502976 | bytes 8388612 | tf_op jit(solution)/shard_map/while/body/eval_jaxpr/gqk,qgd->kd/dot_general | solution.py:48
  210.5 1.9 collective-permute-start.1
  212.5 10.1 %collective-permute-done.1 = bf16[2,1024,128]{2,1,0:T(8,128)(2,1)S(1)} collective-permute-done((bf16[2,1024,128]{2,1,0:T(8,128)(2,1)S(1)}, bf16[2,1024,128]{2,1,0:T(8,128)(2,1)S(1)}, u32[]{:S(2)}, u32[]{:S(2)}) %collective-permute-start.1) | collective-permute-done | bytes 524320 | tf_op jit(solution)/shard_map/ppermute | solution.py:16
  224.7 4.0 %all-to-all-start.7 = ((bf16[64,16,128]{2,0,1:T(8,128)(2,1)}), bf16[64,16,128]{2,0,1:T(8,128)(2,1)S(1)}, u32[]{:S(2)}, u32[]{:S(2)}) async-start(bf16[64,16,128]{2,0,1:T(8,128)(2,1)} %copy.113), calls=%async_computation.7 | async-start | bytes 524288 | tf_op jit(solution)/shard_map/all_to_all | solution.py:151
  229.5 7.2 %all-to-all-done.7 = bf16[64,16,128]{2,0,1:T(8,128)(2,1)S(1)} async-done(((bf16[64,16,128]{2,0,1:T(8,128)(2,1)}), bf16[64,16,128]{2,0,1:T(8,128)(2,1)S(1)}, u32[]{:S(2)}, u32[]{:S(2)}) %all-to-all-start.7) | async-done | bytes 262176 | tf_op jit(solution)/shard_map/all_to_all | solution.py:151
  236.6 5.5 %all-to-all-start.6 = ((bf16[64,16,128]{2,0,1:T(8,128)(2,1)}), bf16[64,16,128]{2,0,1:T(8,128)(2,1)S(1)}, u32[]{:S(2)}, u32[]{:S(2)}) async-start(bf16[64,16,128]{2,0,1:T(8,128)(2,1)} %copy.111), calls=%async_computation.6 | async-start | bytes 524288 | tf_op jit(solution)/shard_map/all_to_all | solution.py:148
  242.2 1.5 reshape.219
  243.7 1.5 copy.106
  245.2 5.0 %all-to-all-done.6 = bf16[64,16,128]{2,0,1:T(8,128)(2,1)S(1)} async-done(((bf16[64,16,128]{2,0,1:T(8,128)(2,1)}), bf16[64,16,128]{2,0,1:T(8,128)(2,1)S(1)}, u32[]{:S(2)}, u32[]{:S(2)}) %all-to-all-start.6) | async-done | bytes 262176 | tf_op jit(solution)/shard_map/all_to_all | solution.py:148
  250.2 5.7 %all-to-all-start.4 = ((bf16[64,16,512]{2,0,1:T(8,128)(2,1)}), bf16[64,16,512]{2,0,1:T(8,128)(2,1)S(1)}, u32[]{:S(2)}, u32[]{:S(2)}) async-start(bf16[64,16,512]{2,0,1:T(8,128)(2,1)} %copy.106), calls=%async_computation.4 | async-start | bytes 2097152 | tf_op jit(solution)/shard_map/all_to_all | solution.py:146
  256.3 1.6 copy.109
  257.9 22.9 %all-to-all-done.4 = bf16[64,16,512]{2,0,1:T(8,128)(2,1)S(1)} async-done(((bf16[64,16,512]{2,0,1:T(8,128)(2,1)}), bf16[64,16,512]{2,0,1:T(8,128)(2,1)S(1)}, u32[]{:S(2)}, u32[]{:S(2)}) %all-to-all-start.4) | async-done | bytes 1048608 | tf_op jit(solution)/shard_map/all_to_all | solution.py:146
  280.8 4.9 %all-to-all-start.5 = ((bf16[64,16,512]{2,0,1:T(8,128)(2,1)}), bf16[64,16,512]{2,0,1:T(8,128)(2,1)S(1)}, u32[]{:S(2)}, u32[]{:S(2)}) async-start(bf16[64,16,512]{2,0,1:T(8,128)(2,1)} %copy.109), calls=%async_computation.5 | async-start | bytes 2097152 | tf_op jit(solution)/shard_map/all_to_all | solution.py:147
  289.1 1.4 copy.134
  290.4 20.1 %all-to-all-done.5 = bf16[64,16,512]{2,0,1:T(8,128)(2,1)S(1)} async-done(((bf16[64,16,512]{2,0,1:T(8,128)(2,1)}), bf16[64,16,512]{2,0,1:T(8,128)(2,1)S(1)}, u32[]{:S(2)}, u32[]{:S(2)}) %all-to-all-start.5) | async-done | bytes 1048608 | tf_op jit(solution)/shard_map/all_to_all | solution.py:147
  311.1 1.4 copy.135
  (68 shorter events, 32.7 us)
Async XLA Ops:
  0.6 69.9 %copy-start.4 = (s32[2048]{0:T(1024)S(1)}, s32[2048]{0:T(1024)}, u32[]{:S(2)}) copy-start(s32[2048]{0:T(1024)} %param.19) | copy-start | bytes 24580
  2.4 14.5 %all-to-all-start = ((bf16[64,16,128]{2,0,1:T(8,128)(2,1)}), bf16[64,16,128]{2,0,1:T(8,128)(2,1)S(1)}, u32[]{:S(2)}, u32[]{:S(2)}) async-start(bf16[64,16,128]{2,0,1:T(8,128)(2,1)} %bitcast.1), calls=%async_computation | async-start | bytes 524288 | tf_op jit(solution)/shard_map/all_to_all | solution.py:82
  16.9 13.5 %all-to-all-start.1 = ((bf16[64,16,128]{2,0,1:T(8,128)(2,1)}), bf16[64,16,128]{2,0,1:T(8,128)(2,1)S(1)}, u32[]{:S(2)}, u32[]{:S(2)}) async-start(bf16[64,16,128]{2,0,1:T(8,128)(2,1)} %bitcast.4), calls=%async_computation.1 | async-start | bytes 524288 | tf_op jit(solution)/shard_map/all_to_all | solution.py:83
  30.4 30.6 %all-to-all-start.2 = ((bf16[64,16,512]{2,0,1:T(8,128)(2,1)}), bf16[64,16,512]{2,0,1:T(8,128)(2,1)S(1)}, u32[]{:S(2)}, u32[]{:S(2)}) async-start(bf16[64,16,512]{2,0,1:T(8,128)(2,1)} %bitcast.11), calls=%async_computation.2 | async-start | bytes 2097152 | tf_op jit(solution)/shard_map/all_to_all | solution.py:80
  61.0 38.6 %all-to-all-start.3 = ((bf16[64,16,512]{2,0,1:T(8,128)(2,1)}), bf16[64,16,512]{2,0,1:T(8,128)(2,1)S(1)}, u32[]{:S(2)}, u32[]{:S(2)}) async-start(bf16[64,16,512]{2,0,1:T(8,128)(2,1)} %bitcast.13), calls=%async_computation.3 | async-start | bytes 2097152 | tf_op jit(solution)/shard_map/all_to_all | solution.py:81
  67.1 27.8 %collective-permute-start = (bf16[2,1024,128]{2,1,0:T(8,128)(2,1)}, bf16[2,1024,128]{2,1,0:T(8,128)(2,1)S(1)}, u32[]{:S(2)}, u32[]{:S(2)}) collective-permute-start(bf16[2,1024,128]{2,1,0:T(8,128)(2,1)} %pad_maximum_fusion), channel_id=1, source_target_pairs={{0,1},{1,2},{2,3},{3,4},{4,5},{5,6},{6,7},{7,8},{8,9},{9,10},{10,1... | collective-permute-start | bytes 1572872 | tf_op jit(solution)/shard_map/ppermute | solution.py:16
  70.5 35.4 %dynamic-slice-start = ((s32[2048]{0:T(1024)}, s32[]{:T(128)}), s32[1024]{0:T(1024)S(1)}, s32[]{:S(2)}) async-start(s32[2048]{0:T(1024)} %param.19, s32[]{:T(128)} %select_n.46), calls=%async_computation.8 | async-start | bytes 8704 | tf_op jit(solution)/shard_map/dynamic_slice | solution.py:96
  120.7 9.1 %copy-start.1 = (bf16[1024,4,128]{2,1,0:T(4,128)(2,1)S(1)}, bf16[1024,4,128]{2,1,0:T(4,128)(2,1)}, u32[]{:S(2)}) copy-start(bf16[1024,4,128]{2,1,0:T(4,128)(2,1)} %get-tuple-element.500) | copy-start | bytes 3145732 | tf_op jit(solution)/shard_map/while
  140.1 2.7 copy-start
  171.8 9.1 %copy-start.1 = (bf16[1024,4,128]{2,1,0:T(4,128)(2,1)S(1)}, bf16[1024,4,128]{2,1,0:T(4,128)(2,1)}, u32[]{:S(2)}) copy-start(bf16[1024,4,128]{2,1,0:T(4,128)(2,1)} %get-tuple-element.500) | copy-start | bytes 3145732 | tf_op jit(solution)/shard_map/while
  191.3 2.7 copy-start
  208.2 47.6 %copy-start.2 = (bf16[1024,4,128]{2,1,0:T(4,128)(2,1)S(1)}, bf16[1024,4,128]{2,1,0:T(4,128)(2,1)}, u32[]{:S(2)}) copy-start(bf16[1024,4,128]{2,1,0:T(4,128)(2,1)} %get-tuple-element.262) | copy-start | bytes 3145732
  210.5 12.0 %collective-permute-start.1 = (bf16[2,1024,128]{2,1,0:T(8,128)(2,1)S(1)}, bf16[2,1024,128]{2,1,0:T(8,128)(2,1)S(1)}, u32[]{:S(2)}, u32[]{:S(2)}) collective-permute-start(bf16[2,1024,128]{2,1,0:T(8,128)(2,1)S(1)} %pad_maximum_fusion.3), channel_id=1, source_target_pairs={{1,0},{2,1},{3,2},{4,3},{5,4},{6,5},{7,6},{8,7},{9,8},{10,9},{11,1... | collective-permute-start | bytes 1572872 | tf_op jit(solution)/shard_map/ppermute | solution.py:16
  224.7 11.9 %all-to-all-start.7 = ((bf16[64,16,128]{2,0,1:T(8,128)(2,1)}), bf16[64,16,128]{2,0,1:T(8,128)(2,1)S(1)}, u32[]{:S(2)}, u32[]{:S(2)}) async-start(bf16[64,16,128]{2,0,1:T(8,128)(2,1)} %copy.113), calls=%async_computation.7 | async-start | bytes 524288 | tf_op jit(solution)/shard_map/all_to_all | solution.py:151
  236.6 13.5 %all-to-all-start.6 = ((bf16[64,16,128]{2,0,1:T(8,128)(2,1)}), bf16[64,16,128]{2,0,1:T(8,128)(2,1)S(1)}, u32[]{:S(2)}, u32[]{:S(2)}) async-start(bf16[64,16,128]{2,0,1:T(8,128)(2,1)} %copy.111), calls=%async_computation.6 | async-start | bytes 524288 | tf_op jit(solution)/shard_map/all_to_all | solution.py:148
  250.2 5.7 %copy-start.3 = (bf16[64,16,128]{2,0,1:T(8,128)(2,1)}, bf16[64,16,128]{2,0,1:T(8,128)(2,1)S(1)}, u32[]{:S(2)}) copy-start(bf16[64,16,128]{2,0,1:T(8,128)(2,1)S(1)} %all-to-all-done.6) | copy-start | bytes 786436
  250.2 30.6 %all-to-all-start.4 = ((bf16[64,16,512]{2,0,1:T(8,128)(2,1)}), bf16[64,16,512]{2,0,1:T(8,128)(2,1)S(1)}, u32[]{:S(2)}, u32[]{:S(2)}) async-start(bf16[64,16,512]{2,0,1:T(8,128)(2,1)} %copy.106), calls=%async_computation.4 | async-start | bytes 2097152 | tf_op jit(solution)/shard_map/all_to_all | solution.py:146
  280.8 29.8 %all-to-all-start.5 = ((bf16[64,16,512]{2,0,1:T(8,128)(2,1)}), bf16[64,16,512]{2,0,1:T(8,128)(2,1)S(1)}, u32[]{:S(2)}, u32[]{:S(2)}) async-start(bf16[64,16,512]{2,0,1:T(8,128)(2,1)} %copy.109), calls=%async_computation.5 | async-start | bytes 2097152 | tf_op jit(solution)/shard_map/all_to_all | solution.py:147
where the time goes:
time: 314 us; the launch traced here: 312 us
  waiting for transfers between devices  123 us (39%)
  local copies, waits for them, and re-layouts  48.3 us (15%)
  starting transfers between devices  48.1 us (15%)
  matrix products  47.9 us (15%)
  other arithmetic  44.5 us (14%)
    ppermute x2, waiting for transfers between devices, shifted(): return lax.ppermute(block, axis, route)  34.5 us
    all_to_all x1, waiting for transfers between devices, on_device(): lax.all_to_all(out_send, 'seq', split_axis=1, concat_axis=1, tiled=True)  22.9 us
    all_to_all x1, waiting for transfers between devices, on_device(): lax.all_to_all(query_send, 'seq', split_axis=1, concat_axis=1, tiled=True)  21.9 us
    all_to_all x1, waiting for transfers between devices, on_device(): lax.all_to_all(dq_send, 'seq', split_axis=1, concat_axis=1, tiled=True)  20.1 us
    sub x2, other arithmetic, attend_block(): weights = jnp.exp(scores - row_max)  20 us
    convert_element_type x2, other arithmetic, attend_block(): probs_low = softmax.astype(jnp.bfloat16)  18.2 us
    dot_general x2, matrix products, attend_block(): jnp.einsum('qgd,kd->gqk', grad_block, value_block, preferred_element_type...  11.7 us
    dot_general x2, matrix products, attend_block(): jnp.einsum('gqk,qgd->kd', probs_low, grad_block, preferred_element_type=j...  11.3 us
  transfers between devices with their start and end apart: 10, of which 9 were waited for; matrix products, arithmetic and copies ran while one was open for 8% of the time, Pallas kernels for 0%

commit v1 on v0

--- a/solution.py
+++ b/solution.py
@@ -8,6 +8,35 @@
 KV = 8
 HD = 128
 MOST = 1024
+
+
+def _show_copies(a0, array_axis, w_in):
+    top, state_next = (a0.shape[:array_axis], a0.shape[array_axis + 1 :])
+    item_now = jnp.moveaxis(a0.reshape(*top, w_in, -1, *state_next), array_axis, 0)
+    return item_now
+
+
+def target_divide(my_data, ndim_at):
+    d_next = list(my_data.shape[1:])
+    d_next[ndim_at] *= my_data.shape[0]
+    val2 = jnp.moveaxis(my_data, 0, ndim_at).reshape(d_next)
+    return val2
+
+
+def recover_entries(vector, link_axis, point, view):
+    everything = lax.axis_index(link_axis)
+    formed = lax.axis_size(link_axis)
+    shaped, inter = (formed, everything)
+    answer = _show_copies(vector, point, shaped)
+    sides = [answer[inter]]
+    for d in range(1, shaped):
+        then = answer[inter ^ d]
+        big = lax.ppermute(then, link_axis, [(rr, rr ^ d) for rr in range(shaped)])
+        sides.append(big)
+    z2 = jnp.stack(sides, axis=0)
+    answer = z2[inter ^ jnp.arange(shaped)]
+    found_now = target_divide(answer, view)
+    return found_now
 
 
 def shifted(block, axis, distance):
@@ -148,13 +177,7 @@
         lax.all_to_all(
             key_own.reshape(slot_rows, devices, HD), "seq", split_axis=1, concat_axis=1, tiled=True
         ),
-        lax.all_to_all(
-            value_own.reshape(slot_rows, devices, HD),
-            "seq",
-            split_axis=1,
-            concat_axis=1,
-            tiled=True,
-        ),
+        recover_entries(value_own.reshape(slot_rows, devices, HD), "seq", 1, 1),
     )
     grad_keys = from_slots(key_back, HD).reshape(local_rows, KV * HD)
     grad_values = from_slots(value_back, HD).reshape(local_rows, KV * HD)

time: 314 us -> 310 us (0.987)
  waiting for transfers between devices: 123 us -> 105 us
  starting transfers between devices: 48.1 us -> 60.3 us
    ppermute x0 -> x15, waiting for transfers between devices: none -> 29.9 us  [recover_entries(): big = lax.ppermute(then, link_axis, [(rr, rr ^ d) for rr in range(shaped)])]
    all_to_all x1, waiting for transfers between devices: 22.9 us -> 0.01 us  [on_device(): lax.all_to_all(out_send, 'seq', split_axis=1, concat_axis=1, tiled=True)]
    ppermute x0 -> x15, starting transfers between devices: none -> 18.4 us  [recover_entries(): big = lax.ppermute(then, link_axis, [(rr, rr ^ d) for rr in range(shaped)])]
    all_to_all x1, waiting for transfers between devices: 20.1 us -> 3.01 us  [on_device(): lax.all_to_all(dq_send, 'seq', split_axis=1, concat_axis=1, tiled=True)]
    all_to_all x1 -> x0, waiting for transfers between devices: 7.18 us -> none  [on_device(): lax.all_to_all(value_own.reshape(slot_rows, devices, HD), 'seq', split_ax...]
    all_to_all x1 -> x0, starting transfers between devices: 3.97 us -> none  [on_device(): lax.all_to_all(value_own.reshape(slot_rows, devices, HD), 'seq', split_ax...]
    unnamed x14 -> x44, local copies, waits for them, and re-layouts: 9.46 us -> 9.65 us
  transfers between devices with their start and end apart: 10 -> 24, of which waited for: 9 -> 11; matrix products, arithmetic and copies ran while one was open for 8% -> 8% of each run, Pallas kernels for 0% -> 0%
where the time goes in v1:
time: 310 us; the launch traced here: 308 us
  waiting for transfers between devices  105 us (34%)
  starting transfers between devices  60.3 us (19%)
  local copies, waits for them, and re-layouts  49.1 us (16%)
  matrix products  47.9 us (15%)
  other arithmetic  44.5 us (14%)
    ppermute x2, waiting for transfers between devices, shifted(): return lax.ppermute(block, axis, route)  34.5 us
    ppermute x15, waiting for transfers between devices, recover_entries(): big = lax.ppermute(then, link_axis, [(rr, rr ^ d) for rr in range(shaped)])  29.9 us
    all_to_all x1, waiting for transfers between devices, on_device(): lax.all_to_all(query_send, 'seq', split_axis=1, concat_axis=1, tiled=True)  21.9 us
    sub x2, other arithmetic, attend_block(): weights = jnp.exp(scores - row_max)  19.9 us
    ppermute x15, starting transfers between devices, recover_entries(): big = lax.ppermute(then, link_axis, [(rr, rr ^ d) for rr in range(shaped)])  18.4 us
    convert_element_type x2, other arithmetic, attend_block(): probs_low = softmax.astype(jnp.bfloat16)  18.2 us
    dot_general x2, matrix products, attend_block(): jnp.einsum('qgd,kd->gqk', grad_block, value_block, preferred_element_type...  11.7 us
    dot_general x2, matrix products, attend_block(): jnp.einsum('gqk,qgd->kd', grad_scores, query_block, preferred_element_typ...  11.3 us
  transfers between devices with their start and end apart: 24, of which 11 were waited for; matrix products, arithmetic and copies ran while one was open for 8% of the time, Pallas kernels for 0%

profile of v1, /device:TPU:11, one launch (start us, length us, event | category | flops | bytes accessed | tf_op | source)
XLA Modules:
  0.0 308.3 jit_solution(15068652751649944935)
XLA Ops:
  2.4 6.6 %all-to-all-start = ((bf16[64,16,128]{2,0,1:T(8,128)(2,1)}), bf16[64,16,128]{2,0,1:T(8,128)(2,1)S(1)}, u32[]{:S(2)}, u32[]{:S(2)}) async-start(bf16[64,16,128]{2,0,1:T(8,128)(2,1)} %bitcast.1), calls=%async_computation | async-start | bytes 524288 | tf_op jit(solution)/shard_map/all_to_all | solution.py:111
  10.7 6.2 %all-to-all-done = bf16[64,16,128]{2,0,1:T(8,128)(2,1)S(1)} async-done(((bf16[64,16,128]{2,0,1:T(8,128)(2,1)}), bf16[64,16,128]{2,0,1:T(8,128)(2,1)S(1)}, u32[]{:S(2)}, u32[]{:S(2)}) %all-to-all-start) | async-done | bytes 262176 | tf_op jit(solution)/shard_map/all_to_all | solution.py:111
  16.9 5.5 %all-to-all-start.1 = ((bf16[64,16,128]{2,0,1:T(8,128)(2,1)}), bf16[64,16,128]{2,0,1:T(8,128)(2,1)S(1)}, u32[]{:S(2)}, u32[]{:S(2)}) async-start(bf16[64,16,128]{2,0,1:T(8,128)(2,1)} %bitcast.4), calls=%async_computation.1 | async-start | bytes 524288 | tf_op jit(solution)/shard_map/all_to_all | solution.py:112
  22.5 1.6 copy.145
  25.4 5.0 %all-to-all-done.1 = bf16[64,16,128]{2,0,1:T(8,128)(2,1)S(1)} async-done(((bf16[64,16,128]{2,0,1:T(8,128)(2,1)}), bf16[64,16,128]{2,0,1:T(8,128)(2,1)S(1)}, u32[]{:S(2)}, u32[]{:S(2)}) %all-to-all-start.1) | async-done | bytes 262176 | tf_op jit(solution)/shard_map/all_to_all | solution.py:112
  30.4 5.7 %all-to-all-start.2 = ((bf16[64,16,512]{2,0,1:T(8,128)(2,1)}), bf16[64,16,512]{2,0,1:T(8,128)(2,1)S(1)}, u32[]{:S(2)}, u32[]{:S(2)}) async-start(bf16[64,16,512]{2,0,1:T(8,128)(2,1)} %bitcast.11), calls=%async_computation.2 | async-start | bytes 2097152 | tf_op jit(solution)/shard_map/all_to_all | solution.py:109
  36.1 1.6 copy.146
  39.1 21.9 %all-to-all-done.2 = bf16[64,16,512]{2,0,1:T(8,128)(2,1)S(1)} async-done(((bf16[64,16,512]{2,0,1:T(8,128)(2,1)}), bf16[64,16,512]{2,0,1:T(8,128)(2,1)S(1)}, u32[]{:S(2)}, u32[]{:S(2)}) %all-to-all-start.2) | async-done | bytes 1048608 | tf_op jit(solution)/shard_map/all_to_all | solution.py:109
  61.0 4.9 %all-to-all-start.3 = ((bf16[64,16,512]{2,0,1:T(8,128)(2,1)}), bf16[64,16,512]{2,0,1:T(8,128)(2,1)S(1)}, u32[]{:S(2)}, u32[]{:S(2)}) async-start(bf16[64,16,512]{2,0,1:T(8,128)(2,1)} %bitcast.13), calls=%async_computation.3 | async-start | bytes 2097152 | tf_op jit(solution)/shard_map/all_to_all | solution.py:110
  67.1 3.3 %collective-permute-start = (bf16[2,1024,128]{2,1,0:T(8,128)(2,1)}, bf16[2,1024,128]{2,1,0:T(8,128)(2,1)S(1)}, u32[]{:S(2)}, u32[]{:S(2)}) collective-permute-start(bf16[2,1024,128]{2,1,0:T(8,128)(2,1)} %pad_maximum_fusion), channel_id=1, source_target_pairs={{0,1},{1,2},{2,3},{3,4},{4,5},{5,6},{6,7},{7,8},{8,9},{9,10},{10,1... | collective-permute-start | bytes 1572872 | tf_op jit(solution)/shard_map/ppermute | solution.py:45
  70.5 24.4 %collective-permute-done = bf16[2,1024,128]{2,1,0:T(8,128)(2,1)S(1)} collective-permute-done((bf16[2,1024,128]{2,1,0:T(8,128)(2,1)}, bf16[2,1024,128]{2,1,0:T(8,128)(2,1)S(1)}, u32[]{:S(2)}, u32[]{:S(2)}) %collective-permute-start) | collective-permute-done | bytes 524320 | tf_op jit(solution)/shard_map/ppermute | solution.py:45
  95.9 1.5 copy.97
  97.4 2.2 reshape.256
  106.0 102.3 %while.24 = (s32[]{:T(128)}, bf16[1024,4,128]{2,1,0:T(4,128)(2,1)}, bf16[1024,4,128]{2,1,0:T(4,128)(2,1)}, f32[2048,128]{1,0:T(8,128)}, f32[2048,128]{1,0:T(8,12...) while((s32[]{:T(128)}, bf16[1024,4,128]{2,1,0:T(4,128)(2,1)}, ...), condition=%wide.region_4.5_spmd.clone, body=%wide.region_0.4_spmd.clone.sunk | while | flops 4874371072 | bytes 147394880 | solution.py:164
  107.2 1.8 fusion.82
  109.2 1.6 fusion.83
  110.8 10.0 %fusion.84 = (f32[4,512]{1,0:T(4,128)S(1)}, f32[4,512,1536]{1,2,0:T(8,128)}) fusion(f32[1536,512,4]{1,0,2:T(8,128)S(1)} %fusion.82, pred[512,1536]{0,1:T(8,128)(4,1)} %fusion.83), kind=kOutput, calls=%fused_computation.123.clone.1 | output fusion | flops 18875904 | bytes 25960448 | tf_op jit(solution)/shard_map/while/body/eval_jaxpr/sub | solution.py:56
  120.7 9.1 %fusion.85 = bf16[4,512,1536]{1,2,0:T(8,128)(2,1)} fusion(f32[4,512,1536]{1,2,0:T(8,128)} %get-tuple-element.468, f32[4,512]{1,0:T(4,128)S(1)} %get-tuple-element.469), kind=kLoop, calls=%fused_computation.14.clone.1 | loop fusion | flops 6291456 | bytes 18882560 | tf_op jit(solution)/shard_map/while/body/eval_jaxpr/convert_element_type | solution.py:58
  130.3 4.0 %multiply_reduce_fusion.2 = (f32[512,4]{0,1:T(4,128)S(1)}, bf16[512,4,128]{0,2,1:T(8,128)(2,1)S(1)}) fusion(bf16[512,4,128]{0,2,1:T(8,128)(2,1)S(1)} %copy.197, bf16[4,512,1536]{1,2,0:T(8,128)(2,1)} %fusion.85, bf16[2048,128]{1,0:T(8,128)(2,1)} %get-tuple-element.511, s32[]{:T(128)S(6)} %select_n.144), kind=kOutput, calls=%fused_computation.29.clone.1 | convolution fusion | flops 806615040 | bytes 7741444 | tf_op jit(solution)/shard_map/while/body/eval_jaxpr/gqk,kd->qgd/dot_general | solution.py:59
  134.3 5.9 %fusion.86 = bf16[4,512,1536]{1,2,0:T(8,128)(2,1)S(1)} fusion(bf16[512,4,128]{0,2,1:T(8,128)(2,1)S(1)} %copy.197, f32[4,512]{1,0:T(4,128)S(1)} %bitcast.286, f32[4,512,1536]{1,2,0:T(8,128)} %get-tuple-element.468, f32[4,512]{1,0:T(4,128)S(1)} %get-tuple-element.469, bf16[2048,128]{1,0:T(8,128)(2,1)} %get-tuple-element.511, s32[]{:T(128)S(6)} %select_n.144), kind=kOutput, calls=%fused_computation.6.clone.1 | convolution fusion | flops 817889280 | bytes 19808260 | tf_op jit(solution)/shard_map/while/body/eval_jaxpr/qgd,kd->gqk/dot_general | solution.py:63
  140.2 2.6 copy-done
  145.8 5.7 %fusion.88 = f32[2048,128]{1,0:T(8,128)} fusion(f32[2048,128]{1,0:T(8,128)} %get-tuple-element.493, s32[]{:T(128)S(6)} %select_n.144, bf16[4,512,1536]{1,2,0:T(8,128)(2,1)} %copy-done, bf16[512,4,128]{2,1,0:T(4,128)(2,1)S(1)} %constant_dynamic-slice_fusion.21), kind=kOutput, calls=%fused_computation.21.clone.1 | convolution fusion | flops 805699584 | bytes 8388612 | tf_op jit(solution)/shard_map/while/body/eval_jaxpr/gqk,qgd->kd/dot_general | solution.py:74
  151.5 5.6 %fusion.89 = f32[2048,128]{1,0:T(8,128)} fusion(f32[2048,128]{1,0:T(8,128)} %get-tuple-element.494, s32[]{:T(128)S(6)} %select_n.144, bf16[4,512,1536]{1,2,0:T(8,128)(2,1)} %fusion.85, bf16[512,4,128]{0,2,1:T(8,128)(2,1)S(1)} %copy.197), kind=kOutput, calls=%fused_computation.23.clone.1 | convolution fusion | flops 805502976 | bytes 8388612 | tf_op jit(solution)/shard_map/while/body/eval_jaxpr/gqk,qgd->kd/dot_general | solution.py:77
  158.3 1.8 fusion.82
  160.3 1.6 fusion.83
  161.9 10.0 %fusion.84 = (f32[4,512]{1,0:T(4,128)S(1)}, f32[4,512,1536]{1,2,0:T(8,128)}) fusion(f32[1536,512,4]{1,0,2:T(8,128)S(1)} %fusion.82, pred[512,1536]{0,1:T(8,128)(4,1)} %fusion.83), kind=kOutput, calls=%fused_computation.123.clone.1 | output fusion | flops 18875904 | bytes 25960448 | tf_op jit(solution)/shard_map/while/body/eval_jaxpr/sub | solution.py:56
  171.8 9.1 %fusion.85 = bf16[4,512,1536]{1,2,0:T(8,128)(2,1)} fusion(f32[4,512,1536]{1,2,0:T(8,128)} %get-tuple-element.468, f32[4,512]{1,0:T(4,128)S(1)} %get-tuple-element.469), kind=kLoop, calls=%fused_computation.14.clone.1 | loop fusion | flops 6291456 | bytes 18882560 | tf_op jit(solution)/shard_map/while/body/eval_jaxpr/convert_element_type | solution.py:58
  181.5 4.0 %multiply_reduce_fusion.2 = (f32[512,4]{0,1:T(4,128)S(1)}, bf16[512,4,128]{0,2,1:T(8,128)(2,1)S(1)}) fusion(bf16[512,4,128]{0,2,1:T(8,128)(2,1)S(1)} %copy.197, bf16[4,512,1536]{1,2,0:T(8,128)(2,1)} %fusion.85, bf16[2048,128]{1,0:T(8,128)(2,1)} %get-tuple-element.511, s32[]{:T(128)S(6)} %select_n.144), kind=kOutput, calls=%fused_computation.29.clone.1 | convolution fusion | flops 806615040 | bytes 7741444 | tf_op jit(solution)/shard_map/while/body/eval_jaxpr/gqk,kd->qgd/dot_general | solution.py:59
  185.4 5.9 %fusion.86 = bf16[4,512,1536]{1,2,0:T(8,128)(2,1)S(1)} fusion(bf16[512,4,128]{0,2,1:T(8,128)(2,1)S(1)} %copy.197, f32[4,512]{1,0:T(4,128)S(1)} %bitcast.286, f32[4,512,1536]{1,2,0:T(8,128)} %get-tuple-element.468, f32[4,512]{1,0:T(4,128)S(1)} %get-tuple-element.469, bf16[2048,128]{1,0:T(8,128)(2,1)} %get-tuple-element.511, s32[]{:T(128)S(6)} %select_n.144), kind=kOutput, calls=%fused_computation.6.clone.1 | convolution fusion | flops 817889280 | bytes 19808260 | tf_op jit(solution)/shard_map/while/body/eval_jaxpr/qgd,kd->gqk/dot_general | solution.py:63
  191.3 2.6 copy-done
  196.9 5.6 %fusion.88 = f32[2048,128]{1,0:T(8,128)} fusion(f32[2048,128]{1,0:T(8,128)} %get-tuple-element.493, s32[]{:T(128)S(6)} %select_n.144, bf16[4,512,1536]{1,2,0:T(8,128)(2,1)} %copy-done, bf16[512,4,128]{2,1,0:T(4,128)(2,1)S(1)} %constant_dynamic-slice_fusion.21), kind=kOutput, calls=%fused_computation.21.clone.1 | convolution fusion | flops 805699584 | bytes 8388612 | tf_op jit(solution)/shard_map/while/body/eval_jaxpr/gqk,qgd->kd/dot_general | solution.py:74
  202.6 5.6 %fusion.89 = f32[2048,128]{1,0:T(8,128)} fusion(f32[2048,128]{1,0:T(8,128)} %get-tuple-element.494, s32[]{:T(128)S(6)} %select_n.144, bf16[4,512,1536]{1,2,0:T(8,128)(2,1)} %fusion.85, bf16[512,4,128]{0,2,1:T(8,128)(2,1)S(1)} %copy.197), kind=kOutput, calls=%fused_computation.23.clone.1 | convolution fusion | flops 805502976 | bytes 8388612 | tf_op jit(solution)/shard_map/while/body/eval_jaxpr/gqk,qgd->kd/dot_general | solution.py:77
  210.5 1.9 collective-permute-start.1
  212.5 10.1 %collective-permute-done.1 = bf16[2,1024,128]{2,1,0:T(8,128)(2,1)S(1)} collective-permute-done((bf16[2,1024,128]{2,1,0:T(8,128)(2,1)S(1)}, bf16[2,1024,128]{2,1,0:T(8,128)(2,1)S(1)}, u32[]{:S(2)}, u32[]{:S(2)}) %collective-permute-start.1) | collective-permute-done | bytes 524320 | tf_op jit(solution)/shard_map/ppermute | solution.py:45
  224.7 4.0 %all-to-all-start.6 = ((bf16[64,16,128]{2,0,1:T(8,128)(2,1)}), bf16[64,16,128]{2,0,1:T(8,128)(2,1)S(1)}, u32[]{:S(2)}, u32[]{:S(2)}) async-start(bf16[64,16,128]{2,0,1:T(8,128)(2,1)} %copy.109), calls=%async_computation.6 | async-start | bytes 524288 | tf_op jit(solution)/shard_map/all_to_all | solution.py:177
  230.2 1.6 copy.107
  231.7 4.9 %all-to-all-done.6 = bf16[64,16,128]{2,0,1:T(8,128)(2,1)S(1)} async-done(((bf16[64,16,128]{2,0,1:T(8,128)(2,1)}), bf16[64,16,128]{2,0,1:T(8,128)(2,1)S(1)}, u32[]{:S(2)}, u32[]{:S(2)}) %all-to-all-start.6) | async-done | bytes 262176 | tf_op jit(solution)/shard_map/all_to_all | solution.py:177
  236.6 5.7 %all-to-all-start.5 = ((bf16[64,16,512]{2,0,1:T(8,128)(2,1)}), bf16[64,16,512]{2,0,1:T(8,128)(2,1)S(1)}, u32[]{:S(2)}, u32[]{:S(2)}) async-start(bf16[64,16,512]{2,0,1:T(8,128)(2,1)} %copy.107), calls=%async_computation.5 | async-start | bytes 2097152 | tf_op jit(solution)/shard_map/all_to_all | solution.py:176
  242.8 1.5 copy.104
  245.9 1.5 collective-permute-start.4
  249.5 2.5 collective-permute-start.8
  252.0 2.1 collective-permute-start.9
  254.2 6.6 %collective-permute-done.5 = bf16[64,1,128]{2,0,1:T(8,128)(2,1)S(1)} collective-permute-done((bf16[64,1,128]{2,0,1:T(8,128)(2,1)S(1)}, bf16[64,1,128]{2,0,1:T(8,128)(2,1)S(1)}, u32[]{:S(2)}, u32[]{:S(2)}) %collective-permute-start.5) | collective-permute-done | bytes 16416 | tf_op jit(solution)/shard_map/ppermute | solution.py:34
  260.8 2.4 collective-permute-start.10
  264.1 1.8 collective-permute-start.12
  265.9 3.0 all-to-all-done.5
  268.9 4.3 %all-to-all-start.4 = ((bf16[64,16,512]{2,0,1:T(8,128)(2,1)}), bf16[64,16,512]{2,0,1:T(8,128)(2,1)S(1)}, u32[]{:S(2)}, u32[]{:S(2)}) async-start(bf16[64,16,512]{2,0,1:T(8,128)(2,1)} %copy.104), calls=%async_computation.4 | async-start | bytes 2097152 | tf_op jit(solution)/shard_map/all_to_all | solution.py:175
  277.8 21.6 %collective-permute-done.13 = bf16[64,1,128]{2,0,1:T(8,128)(2,1)S(1)} collective-permute-done((bf16[64,1,128]{2,0,1:T(8,128)(2,1)S(1)}, bf16[64,1,128]{2,0,1:T(8,128)(2,1)S(1)}, u32[]{:S(2)}, u32[]{:S(2)}) %collective-permute-start.13) | collective-permute-done | bytes 16416 | tf_op jit(solution)/shard_map/ppermute | solution.py:34
  (130 shorter events, 48.7 us)
Async XLA Ops:
  0.6 69.9 %copy-start.4 = (s32[2048]{0:T(1024)S(1)}, s32[2048]{0:T(1024)}, u32[]{:S(2)}) copy-start(s32[2048]{0:T(1024)} %param.19) | copy-start | bytes 24580
  2.4 14.5 %all-to-all-start = ((bf16[64,16,128]{2,0,1:T(8,128)(2,1)}), bf16[64,16,128]{2,0,1:T(8,128)(2,1)S(1)}, u32[]{:S(2)}, u32[]{:S(2)}) async-start(bf16[64,16,128]{2,0,1:T(8,128)(2,1)} %bitcast.1), calls=%async_computation | async-start | bytes 524288 | tf_op jit(solution)/shard_map/all_to_all | solution.py:111
  16.9 13.5 %all-to-all-start.1 = ((bf16[64,16,128]{2,0,1:T(8,128)(2,1)}), bf16[64,16,128]{2,0,1:T(8,128)(2,1)S(1)}, u32[]{:S(2)}, u32[]{:S(2)}) async-start(bf16[64,16,128]{2,0,1:T(8,128)(2,1)} %bitcast.4), calls=%async_computation.1 | async-start | bytes 524288 | tf_op jit(solution)/shard_map/all_to_all | solution.py:112
  30.4 30.6 %all-to-all-start.2 = ((bf16[64,16,512]{2,0,1:T(8,128)(2,1)}), bf16[64,16,512]{2,0,1:T(8,128)(2,1)S(1)}, u32[]{:S(2)}, u32[]{:S(2)}) async-start(bf16[64,16,512]{2,0,1:T(8,128)(2,1)} %bitcast.11), calls=%async_computation.2 | async-start | bytes 2097152 | tf_op jit(solution)/shard_map/all_to_all | solution.py:109
  61.0 38.6 %all-to-all-start.3 = ((bf16[64,16,512]{2,0,1:T(8,128)(2,1)}), bf16[64,16,512]{2,0,1:T(8,128)(2,1)S(1)}, u32[]{:S(2)}, u32[]{:S(2)}) async-start(bf16[64,16,512]{2,0,1:T(8,128)(2,1)} %bitcast.13), calls=%async_computation.3 | async-start | bytes 2097152 | tf_op jit(solution)/shard_map/all_to_all | solution.py:110
  67.1 27.8 %collective-permute-start = (bf16[2,1024,128]{2,1,0:T(8,128)(2,1)}, bf16[2,1024,128]{2,1,0:T(8,128)(2,1)S(1)}, u32[]{:S(2)}, u32[]{:S(2)}) collective-permute-start(bf16[2,1024,128]{2,1,0:T(8,128)(2,1)} %pad_maximum_fusion), channel_id=1, source_target_pairs={{0,1},{1,2},{2,3},{3,4},{4,5},{5,6},{6,7},{7,8},{8,9},{9,10},{10,1... | collective-permute-start | bytes 1572872 | tf_op jit(solution)/shard_map/ppermute | solution.py:45
  70.5 35.5 %dynamic-slice-start = ((s32[2048]{0:T(1024)}, s32[]{:T(128)}), s32[1024]{0:T(1024)S(1)}, s32[]{:S(2)}) async-start(s32[2048]{0:T(1024)} %param.19, s32[]{:T(128)} %select_n.104), calls=%async_computation.7 | async-start | bytes 8704 | tf_op jit(solution)/shard_map/dynamic_slice | solution.py:125
  120.7 9.1 %copy-start.1 = (bf16[1024,4,128]{2,1,0:T(4,128)(2,1)S(1)}, bf16[1024,4,128]{2,1,0:T(4,128)(2,1)}, u32[]{:S(2)}) copy-start(bf16[1024,4,128]{2,1,0:T(4,128)(2,1)} %get-tuple-element.516) | copy-start | bytes 3145732 | tf_op jit(solution)/shard_map/while
  140.2 2.6 copy-start
  171.8 9.1 %copy-start.1 = (bf16[1024,4,128]{2,1,0:T(4,128)(2,1)S(1)}, bf16[1024,4,128]{2,1,0:T(4,128)(2,1)}, u32[]{:S(2)}) copy-start(bf16[1024,4,128]{2,1,0:T(4,128)(2,1)} %get-tuple-element.516) | copy-start | bytes 3145732 | tf_op jit(solution)/shard_map/while
  191.3 2.6 copy-start
  208.2 34.1 %copy-start.2 = (bf16[1024,4,128]{2,1,0:T(4,128)(2,1)S(1)}, bf16[1024,4,128]{2,1,0:T(4,128)(2,1)}, u32[]{:S(2)}) copy-start(bf16[1024,4,128]{2,1,0:T(4,128)(2,1)} %get-tuple-element.261) | copy-start | bytes 3145732
  210.5 12.0 %collective-permute-start.1 = (bf16[2,1024,128]{2,1,0:T(8,128)(2,1)S(1)}, bf16[2,1024,128]{2,1,0:T(8,128)(2,1)S(1)}, u32[]{:S(2)}, u32[]{:S(2)}) collective-permute-start(bf16[2,1024,128]{2,1,0:T(8,128)(2,1)S(1)} %pad_maximum_fusion.3), channel_id=1, source_target_pairs={{1,0},{2,1},{3,2},{4,3},{5,4},{6,5},{7,6},{8,7},{9,8},{10,9},{11,1... | collective-permute-start | bytes 1572872 | tf_op jit(solution)/shard_map/ppermute | solution.py:45
  224.7 11.9 %all-to-all-start.6 = ((bf16[64,16,128]{2,0,1:T(8,128)(2,1)}), bf16[64,16,128]{2,0,1:T(8,128)(2,1)S(1)}, u32[]{:S(2)}, u32[]{:S(2)}) async-start(bf16[64,16,128]{2,0,1:T(8,128)(2,1)} %copy.109), calls=%async_computation.6 | async-start | bytes 524288 | tf_op jit(solution)/shard_map/all_to_all | solution.py:177
  236.6 5.7 %copy-start.3 = (bf16[64,16,128]{2,0,1:T(8,128)(2,1)}, bf16[64,16,128]{2,0,1:T(8,128)(2,1)S(1)}, u32[]{:S(2)}) copy-start(bf16[64,16,128]{2,0,1:T(8,128)(2,1)S(1)} %all-to-all-done.6) | copy-start | bytes 786436
  236.6 32.3 %all-to-all-start.5 = ((bf16[64,16,512]{2,0,1:T(8,128)(2,1)}), bf16[64,16,512]{2,0,1:T(8,128)(2,1)S(1)}, u32[]{:S(2)}, u32[]{:S(2)}) async-start(bf16[64,16,512]{2,0,1:T(8,128)(2,1)} %copy.107), calls=%async_computation.5 | async-start | bytes 2097152 | tf_op jit(solution)/shard_map/all_to_all | solution.py:176
  245.1 4.1 %collective-permute-start.2 = (bf16[64,1,128]{2,0,1:T(8,128)(2,1)S(1)}, bf16[64,1,128]{2,0,1:T(8,128)(2,1)S(1)}, u32[]{:S(2)}, u32[]{:S(2)}) collective-permute-start(bf16[64,1,128]{2,0,1:T(8,128)(2,1)S(1)} %bitcast.302), channel_id=1, source_target_pairs={{0,1},{1,0},{2,3},{3,2},{4,5},{5,4},{6,7},{7,6},{8,9},{9,8},{10,11... | collective-permute-start | bytes 49160 | tf_op jit(solution)/shard_map/ppermute | solution.py:34
  245.6 3.9 %collective-permute-start.3 = (bf16[64,1,128]{2,0,1:T(8,128)(2,1)S(1)}, bf16[64,1,128]{2,0,1:T(8,128)(2,1)S(1)}, u32[]{:S(2)}, u32[]{:S(2)}) collective-permute-start(bf16[64,1,128]{2,0,1:T(8,128)(2,1)S(1)} %bitcast.301), channel_id=1, source_target_pairs={{0,2},{1,3},{2,0},{3,1},{4,6},{5,7},{6,4},{7,5},{8,10},{9,11},{10,... | collective-permute-start | bytes 49160 | tf_op jit(solution)/shard_map/ppermute | solution.py:34
  245.9 6.1 %collective-permute-start.4 = (bf16[64,1,128]{2,0,1:T(8,128)(2,1)S(1)}, bf16[64,1,128]{2,0,1:T(8,128)(2,1)S(1)}, u32[]{:S(2)}, u32[]{:S(2)}) collective-permute-start(bf16[64,1,128]{2,0,1:T(8,128)(2,1)S(1)} %bitcast.300), channel_id=1, source_target_pairs={{0,3},{1,2},{2,1},{3,0},{4,7},{5,6},{6,5},{7,4},{8,11},{9,10},{10,... | collective-permute-start | bytes 49160 | tf_op jit(solution)/shard_map/ppermute | solution.py:34
  247.4 13.4 %collective-permute-start.5 = (bf16[64,1,128]{2,0,1:T(8,128)(2,1)S(1)}, bf16[64,1,128]{2,0,1:T(8,128)(2,1)S(1)}, u32[]{:S(2)}, u32[]{:S(2)}) collective-permute-start(bf16[64,1,128]{2,0,1:T(8,128)(2,1)S(1)} %bitcast.299), channel_id=1, source_target_pairs={{0,4},{1,5},{2,6},{3,7},{4,0},{5,1},{6,2},{7,3},{8,12},{9,13},{10,... | collective-permute-start | bytes 49160 | tf_op jit(solution)/shard_map/ppermute | solution.py:34
  247.7 15.6 %collective-permute-start.6 = (bf16[64,1,128]{2,0,1:T(8,128)(2,1)S(1)}, bf16[64,1,128]{2,0,1:T(8,128)(2,1)S(1)}, u32[]{:S(2)}, u32[]{:S(2)}) collective-permute-start(bf16[64,1,128]{2,0,1:T(8,128)(2,1)S(1)} %bitcast.298), channel_id=1, source_target_pairs={{0,5},{1,4},{2,7},{3,6},{4,1},{5,0},{6,3},{7,2},{8,13},{9,12},{10,... | collective-permute-start | bytes 49160 | tf_op jit(solution)/shard_map/ppermute | solution.py:34
  249.3 14.8 %collective-permute-start.7 = (bf16[64,1,128]{2,0,1:T(8,128)(2,1)S(1)}, bf16[64,1,128]{2,0,1:T(8,128)(2,1)S(1)}, u32[]{:S(2)}, u32[]{:S(2)}) collective-permute-start(bf16[64,1,128]{2,0,1:T(8,128)(2,1)S(1)} %bitcast.297), channel_id=1, source_target_pairs={{0,6},{1,7},{2,4},{3,5},{4,2},{5,3},{6,0},{7,1},{8,14},{9,15},{10,... | collective-permute-start | bytes 49160 | tf_op jit(solution)/shard_map/ppermute | solution.py:34
  249.5 23.8 %collective-permute-start.8 = (bf16[64,1,128]{2,0,1:T(8,128)(2,1)S(1)}, bf16[64,1,128]{2,0,1:T(8,128)(2,1)S(1)}, u32[]{:S(2)}, u32[]{:S(2)}) collective-permute-start(bf16[64,1,128]{2,0,1:T(8,128)(2,1)S(1)} %bitcast.296), channel_id=1, source_target_pairs={{0,7},{1,6},{2,5},{3,4},{4,3},{5,2},{6,1},{7,0},{8,15},{9,14},{10,... | collective-permute-start | bytes 49160 | tf_op jit(solution)/shard_map/ppermute | solution.py:34
  252.0 22.5 %collective-permute-start.9 = (bf16[64,1,128]{2,0,1:T(8,128)(2,1)S(1)}, bf16[64,1,128]{2,0,1:T(8,128)(2,1)S(1)}, u32[]{:S(2)}, u32[]{:S(2)}) collective-permute-start(bf16[64,1,128]{2,0,1:T(8,128)(2,1)S(1)} %bitcast.295), channel_id=1, source_target_pairs={{0,8},{1,9},{2,10},{3,11},{4,12},{5,13},{6,14},{7,15},{8,0},{9,1},... | collective-permute-start | bytes 49160 | tf_op jit(solution)/shard_map/ppermute | solution.py:34
  260.8 14.5 %collective-permute-start.10 = (bf16[64,1,128]{2,0,1:T(8,128)(2,1)S(1)}, bf16[64,1,128]{2,0,1:T(8,128)(2,1)S(1)}, u32[]{:S(2)}, u32[]{:S(2)}) collective-permute-start(bf16[64,1,128]{2,0,1:T(8,128)(2,1)S(1)} %bitcast.294), channel_id=1, source_target_pairs={{0,9},{1,8},{2,11},{3,10},{4,13},{5,12},{6,15},{7,14},{8,1},{9,0},... | collective-permute-start | bytes 49160 | tf_op jit(solution)/shard_map/ppermute | solution.py:34
  263.3 13.2 %collective-permute-start.11 = (bf16[64,1,128]{2,0,1:T(8,128)(2,1)S(1)}, bf16[64,1,128]{2,0,1:T(8,128)(2,1)S(1)}, u32[]{:S(2)}, u32[]{:S(2)}) collective-permute-start(bf16[64,1,128]{2,0,1:T(8,128)(2,1)S(1)} %bitcast.293), channel_id=1, source_target_pairs={{0,10},{1,11},{2,8},{3,9},{4,14},{5,15},{6,12},{7,13},{8,2},{9,3},... | collective-permute-start | bytes 49160 | tf_op jit(solution)/shard_map/ppermute | solution.py:34
  264.1 13.7 %collective-permute-start.12 = (bf16[64,1,128]{2,0,1:T(8,128)(2,1)S(1)}, bf16[64,1,128]{2,0,1:T(8,128)(2,1)S(1)}, u32[]{:S(2)}, u32[]{:S(2)}) collective-permute-start(bf16[64,1,128]{2,0,1:T(8,128)(2,1)S(1)} %bitcast.292), channel_id=1, source_target_pairs={{0,11},{1,10},{2,9},{3,8},{4,15},{5,14},{6,13},{7,12},{8,3},{9,2},... | collective-permute-start | bytes 49160 | tf_op jit(solution)/shard_map/ppermute | solution.py:34
  268.9 37.5 %all-to-all-start.4 = ((bf16[64,16,512]{2,0,1:T(8,128)(2,1)}), bf16[64,16,512]{2,0,1:T(8,128)(2,1)S(1)}, u32[]{:S(2)}, u32[]{:S(2)}) async-start(bf16[64,16,512]{2,0,1:T(8,128)(2,1)} %copy.104), calls=%async_computation.4 | async-start | bytes 2097152 | tf_op jit(solution)/shard_map/all_to_all | solution.py:175
  273.2 26.1 %collective-permute-start.13 = (bf16[64,1,128]{2,0,1:T(8,128)(2,1)S(1)}, bf16[64,1,128]{2,0,1:T(8,128)(2,1)S(1)}, u32[]{:S(2)}, u32[]{:S(2)}) collective-permute-start(bf16[64,1,128]{2,0,1:T(8,128)(2,1)S(1)} %bitcast.291), channel_id=1, source_target_pairs={{0,12},{1,13},{2,14},{3,15},{4,8},{5,9},{6,10},{7,11},{8,4},{9,5},... | collective-permute-start | bytes 49160 | tf_op jit(solution)/shard_map/ppermute | solution.py:34
  274.5 26.4 %collective-permute-start.14 = (bf16[64,1,128]{2,0,1:T(8,128)(2,1)S(1)}, bf16[64,1,128]{2,0,1:T(8,128)(2,1)S(1)}, u32[]{:S(2)}, u32[]{:S(2)}) collective-permute-start(bf16[64,1,128]{2,0,1:T(8,128)(2,1)S(1)} %bitcast.290), channel_id=1, source_target_pairs={{0,13},{1,12},{2,15},{3,14},{4,9},{5,8},{6,11},{7,10},{8,5},{9,4},... | collective-permute-start | bytes 49160 | tf_op jit(solution)/shard_map/ppermute | solution.py:34
  275.3 25.6 %collective-permute-start.15 = (bf16[64,1,128]{2,0,1:T(8,128)(2,1)S(1)}, bf16[64,1,128]{2,0,1:T(8,128)(2,1)S(1)}, u32[]{:S(2)}, u32[]{:S(2)}) collective-permute-start(bf16[64,1,128]{2,0,1:T(8,128)(2,1)S(1)} %bitcast.289), channel_id=1, source_target_pairs={{0,14},{1,15},{2,12},{3,13},{4,10},{5,11},{6,8},{7,9},{8,6},{9,7},... | collective-permute-start | bytes 49160 | tf_op jit(solution)/shard_map/ppermute | solution.py:34
  276.5 24.5 %collective-permute-start.16 = (bf16[64,1,128]{2,0,1:T(8,128)(2,1)S(1)}, bf16[64,1,128]{2,0,1:T(8,128)(2,1)S(1)}, u32[]{:S(2)}, u32[]{:S(2)}) collective-permute-start(bf16[64,1,128]{2,0,1:T(8,128)(2,1)S(1)} %bitcast.288), channel_id=1, source_target_pairs={{0,15},{1,14},{2,13},{3,12},{4,11},{5,10},{6,9},{7,8},{8,7},{9,6},... | collective-permute-start | bytes 49160 | tf_op jit(solution)/shard_map/ppermute | solution.py:34
